TPU v7x, 128 devices: a whole 4x4x4 slice. The times are simulated.
128 devices in a mesh: blk: 8 (over x, core), row: 16 (over z, y).
Axes of the slice: x: 4, y: 4, z: 4, core: 2. Of those that a mesh axis runs over, the one named last changes fastest.
Arguments:
- fibers: bfloat16 [17408, 65536], P(('blk', 'row')), may hold values from -6 to 6
- factor_b: bfloat16 [65536, 256], P('blk'), may hold values from -0.625 to 0.625
- factor_c: bfloat16 [4096, 256], replicated, may hold values from -0.625 to 0.625
- mode2_idx: int32 [17408], P(('blk', 'row')), may hold values from 0 to 8191
- mode3_idx: int32 [17408], P(('blk', 'row')), may hold values from 0 to 4095
- sample_wt: int32 [17408], P(('blk', 'row')), may hold values from 1 to 8
- counts: int32 [128], P(('blk', 'row')), may hold values from 34 to 136, as said below
Outputs:
- factor_new: bfloat16 [65536, 256], P('row')
- leverage: bfloat16 [65536], P('row')
Inputs may be any that keep to these rules, and one draw needn't show every extreme that they name: `counts`: slot s of a device holds a sample when s is under that device's count; other slots carry no sample. The busiest device has all 136 slots live. A sample on blk index b has mode-2 coordinate b * 8192 + mode2_idx.
All inputs are finite; a program needn't handle non-finite values.
Results may differ from a plain program's by a relative error of at most 0.0056.
Values may be sent and summed in bfloat16 or wider, within the bound.
A program may use at most 192 MiB of HBM per device.

v0:
```python
import jax
import jax.numpy as jnp
from jax import lax
from jax.sharding import PartitionSpec as P

ridge_share = 0.05


def build_rows(factor_b, factor_c, row_b, mode3_idx, sample_wt, live):
    product = factor_b[row_b].astype(jnp.float32) * factor_c[mode3_idx].astype(jnp.float32)
    kr_rows = lax.optimization_barrier(product.astype(jnp.bfloat16))
    scale = jnp.where(live, sample_wt.astype(jnp.float32), jnp.float32(0.0))
    weighted = (scale[:, None] * kr_rows.astype(jnp.float32)).astype(jnp.bfloat16)
    return (kr_rows, weighted)


def contract_rows(left, right):
    return lax.dot_general(
        left, right, (((0,), (0,)), ((), ())), preferred_element_type=jnp.float32
    )


def inverse_of(matrix, ridge):
    width = matrix.shape[0]
    identity = jnp.eye(width, dtype=jnp.float32)
    shifted = matrix + ridge * (jnp.trace(matrix) / width) * identity
    lower = jnp.linalg.cholesky(shifted)
    return jax.scipy.linalg.cho_solve((lower, True), identity)


def leverage_of(factor, hinverse, scale):
    wide = factor.astype(jnp.float32)
    quad = jnp.sum(jnp.dot(wide, hinverse, precision=lax.Precision.HIGHEST) * wide, axis=1)
    return (scale * quad).astype(jnp.bfloat16)


def local(fibers, factor_b, factor_c, mode2_idx, mode3_idx, sample_wt, counts):
    slot_cap = fibers.shape[0]
    row_total = fibers.shape[1]
    rank_width = factor_c.shape[1]
    own_live = jnp.arange(slot_cap, dtype=jnp.int32) < counts[0]
    kr_rows, weighted = build_rows(factor_b, factor_c, mode2_idx, mode3_idx, sample_wt, own_live)
    gram = lax.psum(contract_rows(weighted, kr_rows), ("blk", "row"))
    gram_inv = inverse_of(gram, ridge_share)
    group_weighted = lax.all_gather(weighted, "row", axis=0, tiled=True)
    received = lax.all_to_all(fibers, "row", split_axis=1, concat_axis=0, tiled=True)
    partial_value = contract_rows(received, group_weighted)
    scale = row_total / rank_width
    rhs = lax.psum(partial_value, "blk")
    factor = jnp.dot(rhs, gram_inv, precision=lax.Precision.HIGHEST).astype(jnp.bfloat16)
    hmat = lax.psum(contract_rows(factor, factor).astype(jnp.bfloat16), "row").astype(jnp.float32)
    leverage = leverage_of(factor, inverse_of(hmat, 0.0), scale)
    return (factor, leverage)


def solution(mesh):
    placed = (
        P(("blk", "row"), None),
        P("blk", None),
        P(),
        P(("blk", "row")),
        P(("blk", "row")),
        P(("blk", "row")),
        P(("blk", "row")),
    )
    return jax.shard_map(
        local, mesh=mesh, in_specs=placed, out_specs=(P("row", None), P("row")), check_vma=False
    )
```

profile of v0, /device:TPU:1, one launch (start us, length us, event | category | flops | bytes accessed | tf_op | source)
XLA Modules:
  0.0 691.1 jit_solution(9020860313669576720)
XLA Ops:
  8.0 14.8 %copy.41 = bf16[17,16,8,4096]{3,2,0,1:T(8,128)(2,1)} copy(bf16[17,16,8,4096]{3,2,1,0:T(8,128)(2,1)} %bitcast.91) | data formatting | bytes 35651584 | tf_op jit(solution)/shard_map/all_to_all | solution.py:46
  22.8 8.8 %all-to-all-start = ((bf16[136,16,4096]{2,0,1:T(8,128)(2,1)}), bf16[136,16,4096]{2,0,1:T(8,128)(2,1)}, u32[]{:S(2)}, u32[]{:S(2)}) async-start(bf16[136,16,4096]{2,0,1:T(8,128)(2,1)} %bitcast.90), calls=%async_computation | async-start | bytes 35651584 | tf_op jit(solution)/shard_map/all_to_all | solution.py:46
  31.7 0.9 gather_fusion.1
  32.6 3.5 gather_fusion
  36.8 1.0 fusion.33
  37.9 0.7 multiply_convert_fusion
  38.7 362.7 %all-reduce.7.cloned.1.call-done = f32[256,256]{0,1:T(8,128)} async-done(((f32[256,256]{0,1:T(8,128)}), f32[256,256]{0,1:T(8,128)}) %all-reduce.7.cloned.1.call-update) | async-done | bytes 262160 | tf_op jit(solution)/shard_map/psum | solution.py:43
  401.3 1.6 select_reduce_fusion
  403.6 1.0 select_add_fusion
  404.7 1.0 fusion.9
  405.7 11.7 %cholesky.130 = f32[128,128]{1,0:T(8,128)S(1)} custom-call(f32[128,128]{1,0:T(8,128)S(1)} %cholesky.194), custom_call_target="Cholesky" | custom-call | tf_op jit(solution)/shard_map/jit(cholesky)/cholesky | solution.py:27
  417.5 9.8 %custom-call.15 = f32[1,128,128]{1,2,0:T(8,128)S(1)} custom-call(f32[1,128,128]{2,1,0:T(8,128)S(1)} %get-tuple-element.55), custom_call_target="InvertDiagBlocksLowerTriangular" | custom-call | tf_op jit(solution)/shard_map/jit(cholesky)/cholesky | solution.py:27
  427.8 11.7 %cholesky.147 = f32[128,128]{1,0:T(8,128)S(1)} custom-call(f32[128,128]{1,0:T(8,128)S(1)} %convolution_subtract_fusion.5), custom_call_target="Cholesky" | custom-call | tf_op jit(solution)/shard_map/jit(cholesky)/cholesky | solution.py:27
  439.5 0.7 compare_reduce_fusion.2
  441.6 10.9 %convolution_bitcast_fusion = f32[4096,256]{0,1:T(8,128)} fusion(bf16[2176,256]{1,0:T(8,128)(2,1)} %all-gather.2.cloned.1.call-done, bf16[2176,4096]{1,0:T(8,128)(2,1)} %bitcast.2), kind=kOutput, calls=%fused_computation.8 | convolution fusion | flops 4563402752 | bytes 23134208 | tf_op jit(solution)/shard_map/dot_general | solution.py:18
  452.7 3.9 while.4
  452.8 0.6 fusion.59
  453.3 1.4 bitcast_dynamic-update-slice_fusion.4
  454.7 0.6 fusion.59
  455.3 1.4 bitcast_dynamic-update-slice_fusion.4
  456.7 19.7 %custom-call.16 = f32[2,128,128]{1,2,0:T(8,128)S(1)} custom-call(f32[2,128,128]{2,1,0:T(8,128)S(1)} %get-tuple-element.18), custom_call_target="InvertDiagBlocksLowerTriangular" | custom-call | tf_op jit(solution)/shard_map/jit(_cho_solve)/triangular_solve | solution.py:28
  476.4 0.3 fusion.13
  476.7 0.4 convolution_subtract_fusion.3
  477.1 0.3 fusion.23
  477.7 0.3 convolution_subtract_fusion.2
  478.2 42.1 %all-reduce.5.cloned.1.call-done = f32[4096,256]{0,1:T(8,128)} async-done(((f32[4096,256]{0,1:T(8,128)}), f32[4096,256]{0,1:T(8,128)}) %all-reduce.5.cloned.1.call-update) | async-done | bytes 4194320 | tf_op jit(solution)/shard_map/psum | solution.py:49
  520.4 7.1 %convolution_convert_fusion = bf16[4096,256]{0,1:T(8,128)(2,1)S(1)} fusion(f32[4096,256]{0,1:T(8,128)} %all-reduce.5.cloned.1.call-done, f32[128,256]{1,0:T(8,128)S(1)} %fusion.22, f32[128,256]{1,0:T(8,128)S(1)} %fusion.21), kind=kOutput, calls=%fused_computation.9 | convolution fusion | flops 3222339584 | bytes 6553600 | tf_op jit(solution)/shard_map/dot_general | solution.py:50
  527.6 1.4 convolution_convert_fusion.1
  529.0 2.6 copy.34
  531.6 80.3 %all-reduce.9.cloned.1.call-done = bf16[256,256]{0,1:T(8,128)(2,1)} async-done(((bf16[256,256]{0,1:T(8,128)(2,1)}), bf16[256,256]{0,1:T(8,128)(2,1)}) %all-reduce.9.cloned.1.call-update) | async-done | bytes 131088 | tf_op jit(solution)/shard_map/psum | solution.py:51
  611.9 1.6 fusion.1
  614.2 0.9 convert_add_fusion
  615.3 1.0 fusion.8
  616.3 11.7 %cholesky.164 = f32[128,128]{1,0:T(8,128)S(1)} custom-call(f32[128,128]{1,0:T(8,128)S(1)} %cholesky.197), custom_call_target="Cholesky" | custom-call | tf_op jit(solution)/shard_map/jit(cholesky)/cholesky | solution.py:27
  628.0 9.8 %custom-call.17 = f32[1,128,128]{1,2,0:T(8,128)S(1)} custom-call(f32[1,128,128]{2,1,0:T(8,128)S(1)} %get-tuple-element.51), custom_call_target="InvertDiagBlocksLowerTriangular" | custom-call | tf_op jit(solution)/shard_map/jit(cholesky)/cholesky | solution.py:27
  638.3 11.7 %cholesky.181 = f32[128,128]{1,0:T(8,128)S(1)} custom-call(f32[128,128]{1,0:T(8,128)S(1)} %convolution_subtract_fusion.4), custom_call_target="Cholesky" | custom-call | tf_op jit(solution)/shard_map/jit(cholesky)/cholesky | solution.py:27
  650.1 0.6 compare_reduce_fusion.1
  650.7 0.7 compare_reduce_fusion
  652.7 3.9 while.5
  652.7 0.6 fusion.60
  653.3 1.3 bitcast_dynamic-update-slice_fusion.5
  654.7 0.6 fusion.60
  655.2 1.3 bitcast_dynamic-update-slice_fusion.5
  656.6 19.9 %custom-call.18 = f32[2,128,128]{1,2,0:T(8,128)S(1)} custom-call(f32[2,128,128]{2,1,0:T(8,128)S(1)} %get-tuple-element.19), custom_call_target="InvertDiagBlocksLowerTriangular" | custom-call | tf_op jit(solution)/shard_map/jit(_cho_solve)/triangular_solve | solution.py:28
  676.5 0.3 fusion.11
  676.8 0.4 convolution_subtract_fusion.1
  678.4 4.4 fusion
  682.7 0.6 multiply_convert_fusion.2
  (59 shorter events, 3.6 us)
Async XLA Ops:
  8.0 23.7 %copy-start = (bf16[4096,256]{1,0:T(8,128)(2,1)S(1)}, bf16[4096,256]{1,0:T(8,128)(2,1)}, u32[]{:S(2)}) copy-start(bf16[4096,256]{1,0:T(8,128)(2,1)} %param.12) | copy-start | bytes 6291460
  22.8 8.8 %copy-start.3 = (s32[136]{0:T(256)S(1)}, s32[136]{0:T(256)}, u32[]{:S(2)}) copy-start(s32[136]{0:T(256)} %param.14) | copy-start | bytes 1636
  22.8 9.8 %copy-start.4 = (s32[136]{0:T(256)S(1)}, s32[136]{0:T(256)}, u32[]{:S(2)}) copy-start(s32[136]{0:T(256)} %param.13) | copy-start | bytes 1636
  22.8 14.0 %copy-start.5 = (s32[136]{0:T(256)S(1)}, s32[136]{0:T(256)}, u32[]{:S(2)}) copy-start(s32[136]{0:T(256)} %param.15) | copy-start | bytes 1636
  22.8 418.7 %all-to-all-start = ((bf16[136,16,4096]{2,0,1:T(8,128)(2,1)}), bf16[136,16,4096]{2,0,1:T(8,128)(2,1)}, u32[]{:S(2)}, u32[]{:S(2)}) async-start(bf16[136,16,4096]{2,0,1:T(8,128)(2,1)} %bitcast.90), calls=%async_computation | async-start | bytes 35651584 | tf_op jit(solution)/shard_map/all_to_all | solution.py:46
  31.6 369.7 %all-reduce.7.cloned.1.call-start = ((), (), s32[]{:S(2)}) async-start(), calls=%async_computation.3 | async-start | bytes 524288 | tf_op jit(solution)/shard_map/psum | solution.py:43
  37.8 403.7 %all-gather.2.cloned.1.call-start = ((), (), s32[]{:S(2)}) async-start(), calls=%async_computation.1 | async-start | bytes 1183744 | tf_op jit(solution)/shard_map/all_gather | solution.py:45
  38.6 481.8 %all-reduce.5.cloned.1.call-start = ((), (), s32[]{:S(2)}) async-start(), calls=%async_computation.2 | async-start | bytes 8388608 | tf_op jit(solution)/shard_map/psum | solution.py:49
  452.5 159.4 %all-reduce.9.cloned.1.call-start = ((), (), s32[]{:S(2)}) async-start(), calls=%async_computation.4 | async-start | bytes 262144 | tf_op jit(solution)/shard_map/psum | solution.py:51
  527.5 4.0 copy-start.2
  637.8 45.5 %copy-start.1 = (bf16[4096,256]{1,0:T(8,128)(2,1)S(1)}, bf16[4096,256]{1,0:T(8,128)(2,1)}, u32[]{:S(2)}) copy-start(bf16[4096,256]{1,0:T(8,128)(2,1)} %param.12) | copy-start | bytes 6291460
Sparse Core Ops, SparseCore 0:
  37.9 363.3 all-reduce.6
Sparse Core Ops, SparseCore 1:
  40.5 258.4 all-gather.1
  452.6 67.7 all-reduce.4
  529.1 82.8 all-reduce.8
where the time goes:
time: 702 us; the launch traced here: 691 us
  waiting for transfers between devices  485 us (69%)
  other arithmetic  117 us (17%)
  local copies, waits for them, and re-layouts  29.9 us (4%)
  matrix products  29.4 us (4%)
  between operations  20.8 us (3%)
  starting transfers between devices  8.94 us (1%)
    psum x1, waiting for transfers between devices, local(): gram = lax.psum(contract_rows(weighted, kr_rows), ('blk', 'row'))  363 us
    psum x1, waiting for transfers between devices, local(): lax.psum(contract_rows(factor, factor).astype(jnp.bfloat16), 'row')  80.3 us
    another operation x13, other arithmetic, inverse_of(): lower = jnp.linalg.cholesky(shifted)  68.6 us
    psum x1, waiting for transfers between devices, local(): rhs = lax.psum(partial_value, 'blk')  42.1 us
    another operation x5, other arithmetic, inverse_of(): return jax.scipy.linalg.cho_solve((lower, True), identity)  39.6 us
    all_to_all x1, local copies, waits for them, and re-layouts, local(): lax.all_to_all(fibers, 'row', split_axis=1, concat_axis=0, tiled=True)  14.8 us
  transfers between devices with their start and end apart: 5, of which 3 were waited for; matrix products, arithmetic and copies ran while one was open for 10% of the time, Pallas kernels for 0%

commit v1 on v0

v1 whole, which is shorter than its diff:
```python
import jax
import jax.numpy as jnp
from jax import lax
from jax.experimental import pallas as pl
from jax.experimental.pallas import tpu as pltpu
from jax.sharding import PartitionSpec as P

ridge_share = 0.05
MESH = pl.DeviceIdType.MESH
F32 = jnp.float32
BF16 = jnp.bfloat16

ORDER = ((0, 1, 2), (1, 2, 0), (2, 0, 1))
R0 = (0, 96, 176)
RC = (96, 80, 80)
STEPS = (2, 1, 3, 0)
SUB = 512


def block_order():
    seen, order, marks = set(), [], []

    def add(color, d1, d2):
        for d3 in range(4):
            off = [0, 0, 0]
            off[ORDER[color][0]], off[ORDER[color][1]], off[ORDER[color][2]] = d1, d2, d3
            if tuple(off) not in seen:
                seen.add(tuple(off))
                order.append(tuple(off))

    for d2 in STEPS:
        for group in ((2,), (1, 3), (0,)):
            for d1 in group:
                for color in range(3):
                    add(color, d1, d2)
            marks.append(len(order))
    return order, marks


BLOCKS, MARKS = block_order()
PACK = 5


def block_at(t, me):
    code = jnp.int32(0)
    for g in range(0, 64, PACK):
        word = 0
        for j, (dx, dy, dz) in enumerate(BLOCKS[g:g + PACK]):
            word += (dx + 4 * dy + 16 * dz) << (6 * j)
        code = jnp.where(t // PACK == g // PACK, jnp.int32(word), code)
    code = lax.shift_right_logical(code, 6 * (t % PACK)) % 64
    return ((me[0] + code % 4) % 4, (me[1] + code // 4 % 4) % 4, (me[2] + code // 16) % 4)


def position():
    b, r = lax.axis_index("blk"), lax.axis_index("row")
    return (b // 2, r % 4, r // 4), b % 2


def device(coord, core):
    return {"blk": 2 * coord[0] + core, "row": 4 * coord[2] + coord[1]}


def shifted(me, axis, by):
    out = list(me)
    out[axis] = (me[axis] + by) % 4
    return tuple(out)


def reduce_kernel(fib, wt_own, out, fo, fp, wt_far, part, r1, r2, r3, tot,
                  fo_sem, fs_sem, fr_sem, w_sem, s1, v1, s2, v2, s3, v3):
    me, core = position()
    peers = [device(shifted(me, a, s), core) for a in range(3) for s in (1, 3)]
    partner = device(me, 1 - core)
    barrier = pltpu.get_barrier_semaphore()
    for p in peers + [partner]:
        pl.semaphore_signal(barrier, inc=1, device_id=p, device_id_type=MESH)
    pl.semaphore_wait(barrier, 7)

    def column(t, k):
        x, y, z = block_at(t, me)
        return pl.multiple_of((4 * z + y) * 4096 + (2 * x + k) * SUB, SUB)

    def local_copy(t):
        return pltpu.make_async_copy(fib.at[:, pl.ds(column(t, core), SUB)], fo.at[t], fo_sem.at[t])

    def far_copy(t):
        return pltpu.make_async_remote_copy(
            fib.at[:, pl.ds(column(t, 1 - core), SUB)], fp.at[t], fs_sem.at[t], fr_sem.at[t],
            device_id=partner, device_id_type=MESH)

    wt_copy = pltpu.make_async_remote_copy(
        wt_own, wt_far, w_sem.at[0], w_sem.at[1], device_id=partner, device_id_type=MESH)
    wt_copy.start()

    @pl.loop(0, 64)
    def _(t):
        local_copy(t).start()
        far_copy(t).start()

    wt_copy.wait()

    def compute(lo, hi):
        @pl.loop(lo, hi)
        def _(t):
            local_copy(t).wait()
            far_copy(t).wait_recv()
            x, y, z = block_at(t, me)
            acc = jnp.dot(wt_own[...], fo[t], preferred_element_type=F32)
            acc += jnp.dot(wt_far[...], fp[t], preferred_element_type=F32)
            part[x, y, z] = acc.astype(BF16)

    def rank(c):
        return pl.ds(R0[c], RC[c])

    def place(c, i1, i2, i3):
        at = [None] * 3
        at[ORDER[c][0]], at[ORDER[c][1]], at[ORDER[c][2]] = i1, i2, i3
        return tuple(at)

    def half_of(kind, d):
        return d if kind < 2 else 1 - d

    def dest_step(kind, d):
        return 2 if kind == 0 else (1, 3)[d]

    def slab1(c, d1, e, h):
        i1 = (me[ORDER[c][0]] + d1) % 4
        i2 = (me[ORDER[c][1]] + e) % 4
        return place(c, i1, i2, pl.ds(2 * h, 2)) + (rank(c), slice(None))

    def msg1(kind, d, i, c):
        if kind == 1:
            src = r1.at[0, d, i, :, rank(c)]
        else:
            src = part.at[slab1(c, dest_step(kind, d), STEPS[i], half_of(kind, d))]
        return pltpu.make_async_remote_copy(
            src, r1.at[kind, d, i, :, rank(c)], s1.at[kind, d, i, c], v1.at[kind, d, i, c],
            device_id=device(shifted(me, ORDER[c][0], (1, 3)[d]), core), device_id_type=MESH)

    def slab2(c, e, h):
        return slab1(c, 0, e, h)

    def msg2(kind, d, c):
        if kind == 1:
            src = r2.at[0, d, :, rank(c)]
        else:
            src = part.at[slab2(c, dest_step(kind, d), half_of(kind, d))]
        return pltpu.make_async_remote_copy(
            src, r2.at[kind, d, :, rank(c)], s2.at[kind, d, c], v2.at[kind, d, c],
            device_id=device(shifted(me, ORDER[c][1], (1, 3)[d]), core), device_id_type=MESH)

    def lanes(h):
        return pl.ds(h * (SUB // 2), SUB // 2)

    def msg3(kind, d, c):
        if kind == 1:
            src = r3.at[0, d, rank(c)]
        else:
            f = (me[ORDER[c][2]] + dest_step(kind, d)) % 4
            src = tot.at[f, rank(c), lanes(half_of(kind, d))]
        return pltpu.make_async_remote_copy(
            src, r3.at[kind, d, rank(c)], s3.at[kind, d, c], v3.at[kind, d, c],
            device_id=device(shifted(me, ORDER[c][2], (1, 3)[d]), core), device_id_type=MESH)

    def rows16(c, body):
        @pl.loop(0, RC[c] // 16)
        def _(j):
            body(pl.ds(pl.multiple_of(R0[c] + 16 * j, 16), 16))

    def forward1(d, i, c):
        msg1(0, d, i, c).wait_recv()
        at = slab1(c, (1, 3)[d], STEPS[i], d)

        def body(rows):
            mine = part[at[:3] + (rows, slice(None))].astype(F32)
            r1[0, d, i, :, rows] = (r1[0, d, i, :, rows].astype(F32) + mine).astype(BF16)

        rows16(c, body)
        msg1(1, d, i, c).start()

    def finish1(i, c):
        for d in range(2):
            msg1(2, d, i, c).wait_recv()
        for d in range(2):
            msg1(1, d, i, c).wait_recv()
        for h in range(2):
            at = slab1(c, 0, STEPS[i], h)

            def body(rows):
                total = (r1[1, h, i, :, rows].astype(F32) + r1[2, 1 - h, i, :, rows].astype(F32)
                         + part[at[:3] + (rows, slice(None))].astype(F32))
                if STEPS[i] == 0:
                    tot[pl.ds(2 * h, 2), rows] = total
                else:
                    part[at[:3] + (rows, slice(None))] = total.astype(BF16)

            rows16(c, body)

    def forward2(d, c):
        msg2(0, d, c).wait_recv()
        at = slab2(c, (1, 3)[d], d)

        def body(rows):
            mine = part[at[:3] + (rows, slice(None))].astype(F32)
            r2[0, d, :, rows] = (r2[0, d, :, rows].astype(F32) + mine).astype(BF16)

        rows16(c, body)
        msg2(1, d, c).start()

    compute(0, MARKS[0])
    for c in range(3):
        for d in range(2):
            msg1(0, d, 0, c).start()
    compute(MARKS[0], MARKS[1])
    for c in range(3):
        for d in range(2):
            msg1(2, d, 0, c).start()
    compute(MARKS[1], 64)

    for i in range(4):
        for c in range(3):
            for d in range(2):
                forward1(d, i, c)
        if i < 3:
            for kind in (0, 2):
                for c in range(3):
                    for d in range(2):
                        msg1(kind, d, i + 1, c).start()
        for c in range(3):
            finish1(i, c)
            if i == 0:
                for d in range(2):
                    msg2(0, d, c).start()
            elif i < 3:
                d = i - 1
                msg2(2, d, c).start()
                forward2(d, c)

    for c in range(3):
        for d in range(2):
            msg2(2, d, c).wait_recv()
            msg2(1, d, c).wait_recv()
        for h in range(2):
            def body(rows):
                tot[pl.ds(2 * h, 2), rows] += r2[1, h, :, rows].astype(F32) + r2[2, 1 - h, :, rows].astype(F32)

            rows16(c, body)
        for kind in (0, 2):
            for d in range(2):
                msg3(kind, d, c).start()
    for c in range(3):
        for d in range(2):
            msg3(0, d, c).wait_recv()
            f = (me[ORDER[c][2]] + (1, 3)[d]) % 4

            def body(rows):
                r3[0, d, rows] += tot[f, rows, lanes(d)]

            rows16(c, body)
            msg3(1, d, c).start()
    for c in range(3):
        for d in range(2):
            msg3(2, d, c).wait_recv()
            msg3(1, d, c).wait_recv()
        own = me[ORDER[c][2]]
        for h in range(2):
            def body(rows):
                out[rows, lanes(h)] = tot[own, rows, lanes(h)] + r3[1, h, rows] + r3[2, 1 - h, rows]

            rows16(c, body)

    for c in range(3):
        for kind in range(3):
            for d in range(2):
                for i in range(4):
                    msg1(kind, d, i, c).wait_send()
                msg2(kind, d, c).wait_send()
                msg3(kind, d, c).wait_send()

    @pl.loop(0, 64)
    def _(t):
        far_copy(t).wait_send()


def reduce_rhs(fibers, weighted_t):
    cap = fibers.shape[0]
    dma = pltpu.SemaphoreType.DMA
    vmem = pltpu.VMEM
    return pl.pallas_call(
        reduce_kernel,
        name="reduce_rhs",
        out_shape=jax.ShapeDtypeStruct((256, SUB), F32),
        in_specs=[pl.BlockSpec(memory_space=pl.ANY), pl.BlockSpec(memory_space=pltpu.VMEM)],
        out_specs=pl.BlockSpec(memory_space=pltpu.VMEM),
        scratch_shapes=[
            vmem((64, cap, SUB), BF16), vmem((64, cap, SUB), BF16), vmem((256, cap), BF16),
            vmem((4, 4, 4, 256, SUB), BF16),
            vmem((3, 2, 4, 2, 256, SUB), BF16), vmem((3, 2, 2, 256, SUB), BF16),
            vmem((3, 2, 256, SUB // 2), F32), vmem((4, 256, SUB), F32),
            dma((64,)), dma((64,)), dma((64,)), dma((2,)),
            dma((3, 2, 4, 3)), dma((3, 2, 4, 3)), dma((3, 2, 3)), dma((3, 2, 3)), dma((3, 2, 3)), dma((3, 2, 3)),
        ],
        compiler_params=pltpu.CompilerParams(
            collective_id=0, has_side_effects=True, vmem_limit_bytes=60 * 1024 * 1024),
    )(fibers, weighted_t)


def build_rows(factor_b, factor_c, row_b, mode3_idx, sample_wt, live):
    product = factor_b[row_b].astype(F32) * factor_c[mode3_idx].astype(F32)
    kr_rows = lax.optimization_barrier(product.astype(BF16))
    scale = jnp.where(live, sample_wt.astype(F32), F32(0.0))
    weighted = (scale[:, None] * kr_rows.astype(F32)).astype(BF16)
    return (kr_rows, weighted)


def contract_rows(left, right):
    return lax.dot_general(left, right, (((0,), (0,)), ((), ())), preferred_element_type=F32)


def inverse_of(matrix, ridge):
    width = matrix.shape[0]
    identity = jnp.eye(width, dtype=F32)
    shifted_m = matrix + ridge * (jnp.trace(matrix) / width) * identity
    lower = jnp.linalg.cholesky(shifted_m)
    return jax.scipy.linalg.cho_solve((lower, True), identity)


def local(fibers, factor_b, factor_c, mode2_idx, mode3_idx, sample_wt, counts):
    slot_cap, row_total = fibers.shape
    rank_width = factor_c.shape[1]
    own_live = jnp.arange(slot_cap, dtype=jnp.int32) < counts[0]
    kr_rows, weighted = build_rows(factor_b, factor_c, mode2_idx, mode3_idx, sample_wt, own_live)
    gram = lax.psum(contract_rows(weighted, kr_rows), ("blk", "row"))
    gram_inv = inverse_of(gram, ridge_share)
    rhs_t = reduce_rhs(fibers, weighted.T)
    factor_own = lax.dot_general(
        rhs_t, gram_inv, (((0,), (0,)), ((), ())), precision=lax.Precision.HIGHEST).astype(BF16)
    factor = lax.all_gather(factor_own, "blk", axis=0, tiled=True)
    smat = lax.psum(jnp.dot(rhs_t, rhs_t.T, precision=lax.Precision.HIGHEST), ("blk", "row"))
    sinv = inverse_of(smat, 0.0)
    quad = jnp.sum(jnp.dot(sinv, rhs_t, precision=lax.Precision.HIGHEST) * rhs_t, axis=0)
    lev_own = ((row_total / rank_width) * quad).astype(BF16)
    leverage = lax.all_gather(lev_own, "blk", axis=0, tiled=True)
    return (factor, leverage)


def solution(mesh):
    placed = (
        P(("blk", "row"), None),
        P("blk", None),
        P(),
        P(("blk", "row")),
        P(("blk", "row")),
        P(("blk", "row")),
        P(("blk", "row")),
    )
    return jax.shard_map(
        local, mesh=mesh, in_specs=placed, out_specs=(P("row", None), P("row")), check_vma=False
    )
```

time: 702 us -> 433 us (0.62); the launches traced: 691 us -> 432 us
  waiting for transfers between devices: 485 us -> 147 us
  Pallas kernels: 0 us -> 99.4 us
  matrix products: 29.4 us -> 12.1 us
  local copies, waits for them, and re-layouts: 29.9 us -> 17.3 us
  blocking collectives: 0 us -> 11.6 us
  starting transfers between devices: 8.94 us -> 0.46 us
  other arithmetic: 117 us -> 125 us
    psum x1, waiting for transfers between devices: 363 us -> 147 us  [local(): gram = lax.psum(contract_rows(weighted, kr_rows), ('blk', 'row'))]
    psum x2 -> x0, waiting for transfers between devices: 122 us -> none  [the longest x1 80.3 us: local(): lax.psum(contract_rows(factor, factor).astype(jnp.bfloat16), 'row')]
    pallas_call x0 -> x1, Pallas kernels: none -> 99.4 us  [reduce_rhs(): pl.pallas_call(reduce_kernel, name='reduce_rhs', out_shape=jax.ShapeDtype...]
    all_to_all x1 -> x0, local copies, waits for them, and re-layouts: 14.8 us -> none  [local(): lax.all_to_all(fibers, 'row', split_axis=1, concat_axis=0, tiled=True)]
    dot_general x3 -> x1, matrix products: 13.3 us -> 0.93 us  [contract_rows(): lax.dot_general(left, right, (((0,), (0,)), ((), ())), preferred_element_...]
    all_gather x0 -> x1, blocking collectives: none -> 11.6 us  [local(): leverage = lax.all_gather(lev_own, 'blk', axis=0, tiled=True)]
    another operation x13 -> x14, other arithmetic: 68.6 us -> 78.8 us  [inverse_of(): lower = jnp.linalg.cholesky(shifted_m)]
    all_to_all x1 -> x0, starting transfers between devices: 8.77 us -> none  [local(): lax.all_to_all(fibers, 'row', split_axis=1, concat_axis=0, tiled=True)]
  transfers between devices with their start and end apart: 5 -> 2, of which waited for: 3 -> 1; matrix products, arithmetic and copies ran while one was open for 10% -> 12% of each run, Pallas kernels for 0% -> 0%
where the time goes in v1:
time: 433 us; the launch traced here: 432 us
  waiting for transfers between devices  147 us (34%)
  other arithmetic  125 us (29%)
  Pallas kernels  99.4 us (23%)
  between operations  19.4 us (4%)
  local copies, waits for them, and re-layouts  17.3 us (4%)
  matrix products  12.1 us (3%)
  blocking collectives  11.6 us (3%)
    psum x1, waiting for transfers between devices, local(): gram = lax.psum(contract_rows(weighted, kr_rows), ('blk', 'row'))  147 us
    pallas_call x1, Pallas kernels, reduce_rhs(): pl.pallas_call(reduce_kernel, name='reduce_rhs', out_shape=jax.ShapeDtype...  99.4 us
    another operation x14, other arithmetic, inverse_of(): lower = jnp.linalg.cholesky(shifted_m)  78.8 us
    another operation x5, other arithmetic, inverse_of(): return jax.scipy.linalg.cho_solve((lower, True), identity)  39.6 us
    all_gather x1, blocking collectives, local(): leverage = lax.all_gather(lev_own, 'blk', axis=0, tiled=True)  11.6 us
  transfers between devices with their start and end apart: 2, of which 1 were waited for; matrix products, arithmetic and copies ran while one was open for 12% of the time, Pallas kernels for 0%

profile of v1, /device:TPU:1, one launch (start us, length us, event | category | flops | bytes accessed | tf_op | source)
XLA Modules:
  0.0 432.5 jit_solution(4689168118456439349)
XLA Ops:
  8.0 0.7 compare_select_fusion.1
  8.7 0.7 compare_select_fusion
  9.4 0.9 gather_fusion.1
  10.4 3.5 gather_fusion
  14.1 0.7 fusion.11.wt_own
  14.7 0.9 fusion.10
  15.7 99.4 %reduce_rhs.1 = f32[256,512]{1,0:T(8,128)} custom-call(bf16[136,65536]{1,0:T(8,128)(2,1)} %fib.1, bf16[256,136]{1,0:T(8,128)(2,1)} %fusion.11.wt_own), custom_call_target="tpu_custom_call" | custom-call | tf_op jit(solution)/shard_map/reduce_rhs/pallas_call | solution.py:290
  115.1 2.5 fusion.37
  117.6 0.4 all-gather.3.cloned.1.call-start
  118.1 147.2 %all-reduce.4.cloned.1.call-done = (f32[256,256]{0,1:T(8,128)}, f32[256,256]{0,1:T(8,128)}) async-done(((f32[256,256]{0,1:T(8,128)}, f32[256,256]{0,1:T(8,128)}), (f32[256,256]{0,1:T(8,128)}, f32[256,256]{0,1:T(8,128)})) %all-reduce.4.cloned.1.call-update) | async-done | bytes 524304 | tf_op jit(solution)/shard_map/psum | solution.py:334
  265.3 1.6 select_reduce_fusion
  266.9 1.7 select_reduce_fusion.1
  269.9 1.1 select_add_fusion
  271.1 0.7 copy-done.2
  271.9 11.7 %cholesky.164 = f32[128,128]{1,0:T(8,128)S(1)} custom-call(f32[128,128]{1,0:T(8,128)S(1)} %cholesky.197), custom_call_target="Cholesky" | custom-call | tf_op jit(solution)/shard_map/jit(cholesky)/cholesky | solution.py:325
  283.8 11.7 %cholesky.130 = f32[128,128]{1,0:T(8,128)S(1)} custom-call(f32[128,128]{1,0:T(8,128)S(1)} %cholesky.194), custom_call_target="Cholesky" | custom-call | tf_op jit(solution)/shard_map/jit(cholesky)/cholesky | solution.py:325
  295.5 0.6 compare_reduce_fusion.3
  296.2 9.8 %custom-call.15 = f32[1,128,128]{1,2,0:T(8,128)S(1)} custom-call(f32[1,128,128]{2,1,0:T(8,128)S(1)} %get-tuple-element.49), custom_call_target="InvertDiagBlocksLowerTriangular" | custom-call | tf_op jit(solution)/shard_map/jit(cholesky)/cholesky | solution.py:325
  306.5 21.3 %cholesky.147 = f32[128,128]{1,0:T(8,128)S(1)} custom-call(f32[128,128]{1,0:T(8,128)S(1)} %convolution_subtract_fusion.5), custom_call_target="Cholesky" | custom-call | tf_op jit(solution)/shard_map/jit(cholesky)/cholesky | solution.py:325
  327.8 0.7 compare_reduce_fusion.2
  330.0 4.1 while.4
  330.0 0.6 fusion.59
  330.6 1.4 bitcast_dynamic-update-slice_fusion.4
  332.1 0.6 fusion.59
  332.7 1.4 bitcast_dynamic-update-slice_fusion.4
  334.1 19.7 %custom-call.16 = f32[2,128,128]{1,2,0:T(8,128)S(1)} custom-call(f32[2,128,128]{2,1,0:T(8,128)S(1)} %get-tuple-element.18), custom_call_target="InvertDiagBlocksLowerTriangular" | custom-call | tf_op jit(solution)/shard_map/jit(_cho_solve)/triangular_solve | solution.py:326
  353.8 0.3 fusion.15
  354.1 0.4 convolution_subtract_fusion.3
  355.7 1.7 convolution_convert_fusion
  357.4 9.8 %custom-call.17 = f32[1,128,128]{1,2,0:T(8,128)S(1)} custom-call(f32[1,128,128]{2,1,0:T(8,128)S(1)} %get-tuple-element.45), custom_call_target="InvertDiagBlocksLowerTriangular" | custom-call | tf_op jit(solution)/shard_map/jit(cholesky)/cholesky | solution.py:325
  367.3 1.0 constant_dynamic-update-slice_fusion.1
  368.3 1.1 convolution_subtract_fusion.4
  369.4 11.7 %cholesky.181 = f32[128,128]{1,0:T(8,128)S(1)} custom-call(f32[128,128]{1,0:T(8,128)S(1)} %convolution_subtract_fusion.4), custom_call_target="Cholesky" | custom-call | tf_op jit(solution)/shard_map/jit(cholesky)/cholesky | solution.py:325
  381.1 0.6 compare_reduce_fusion.1
  381.8 0.6 compare_reduce_fusion
  383.8 3.9 while.5
  383.8 0.6 fusion.60
  384.4 1.4 bitcast_dynamic-update-slice_fusion.5
  385.8 0.6 fusion.60
  386.4 1.4 bitcast_dynamic-update-slice_fusion.5
  387.7 19.9 %custom-call.18 = f32[2,128,128]{1,2,0:T(8,128)S(1)} custom-call(f32[2,128,128]{2,1,0:T(8,128)S(1)} %get-tuple-element.19), custom_call_target="InvertDiagBlocksLowerTriangular" | custom-call | tf_op jit(solution)/shard_map/jit(_cho_solve)/triangular_solve | solution.py:326
  407.6 0.3 fusion.13
  407.9 0.4 convolution_subtract_fusion.1
  408.9 0.3 convolution_subtract_fusion
  409.5 0.6 fusion
  410.1 11.6 %all-gather = bf16[8,1,512]{2,1,0:T(2,128)(2,1)S(1)} all-gather(bf16[1,1,512]{2,1,0:T(2,128)(2,1)S(1)} %reshape.64), channel_id=1, replica_groups=mesh['blk'=8,'row'=16] {'blk'}, dimensions={0}, use_global_device_ids=true | all-gather | bytes 9216 | tf_op jit(solution)/shard_map/all_gather | solution.py:344
  421.8 0.6 copy.41
  422.4 3.0 copy.68
  (52 shorter events, 3.6 us)
Async XLA Ops:
  7.2 2.2 copy-start
  7.2 6.9 %copy-start.3 = (s32[136]{0:T(256)S(1)}, s32[136]{0:T(256)}, u32[]{:S(2)}) copy-start(s32[136]{0:T(256)} %param.15) | copy-start | bytes 1636
  7.2 258.1 %all-reduce.4.cloned.1.call-start = ((), (), s32[]{:S(2)}) async-start(), calls=%async_computation.1 | async-start | bytes 1048576 | tf_op jit(solution)/shard_map/psum | solution.py:334
  117.6 304.7 %all-gather.3.cloned.1.call-start = ((), (), s32[]{:S(2)}) async-start(), calls=%async_computation | async-start | bytes 2359296 | tf_op jit(solution)/shard_map/all_gather | solution.py:339
  271.1 0.7 copy-start.2
  306.2 49.5 %copy-start.1 = (f32[256,512]{1,0:T(8,128)S(1)}, f32[256,512]{1,0:T(8,128)}, u32[]{:S(2)}) copy-start(f32[256,512]{1,0:T(8,128)} %reduce_rhs.1) | copy-start | bytes 1572868
Sparse Core Ops, SparseCore 0:
  117.7 147.4 all-reduce.3
  357.5 24.6 all-gather.2

commit v2 on v1

--- a/solution.py
+++ b/solution.py
@@ -67,15 +67,101 @@
     return tuple(out)
 
 
-def reduce_kernel(fib, wt_own, out, fo, fp, wt_far, part, r1, r2, r3, tot,
-                  fo_sem, fs_sem, fr_sem, w_sem, s1, v1, s2, v2, s3, v3):
+def all_reduce_phases(part, res, near, rx, ry, rz, far_s, far_v, snd, rcv, me, core):
+    half = core * 128
+    row_x = half + 32 * me[0]
+    row_y = row_x + 8 * me[1]
+    partner = device(me, 1 - core)
+
+    def rows(at, n):
+        return pl.ds(pl.multiple_of(at, 8), n)
+
+    def spread(phase, axis, src_of, dst_of):
+        copies = []
+        for by in (1, 2, 3):
+            to = shifted(me, axis, by)
+            copies.append(pltpu.make_async_remote_copy(
+                src_of(to[axis]), dst_of(by), snd.at[phase, by - 1], rcv.at[phase, by - 1],
+                device_id=device(to, core), device_id_type=MESH))
+        return copies
+
+    def pair(slot, src, dst):
+        return pltpu.make_async_remote_copy(
+            src, dst, far_s.at[slot], far_v.at[slot], device_id=partner, device_id_type=MESH)
+
+    def begin(copies):
+        for copy in copies:
+            copy.start()
+
+    def arrive(copies):
+        for copy in copies:
+            copy.wait_recv()
+
+    first = [pair(0, part.at[rows((1 - core) * 128, 128)], near)]
+    over_x = spread(0, 0, lambda i: part.at[rows(half + 32 * i, 32)], lambda by: rx.at[by - 1])
+    over_y = spread(1, 1, lambda i: part.at[rows(row_x + 8 * i, 8)], lambda by: ry.at[by - 1])
+    over_z = spread(2, 2, lambda i: part.at[rows(row_y, 8)], lambda by: rz.at[me[2]])
+    back_y = spread(3, 1, lambda i: res.at[rows(row_y, 8)], lambda by: res.at[rows(row_y, 8)])
+    back_x = spread(4, 0, lambda i: res.at[rows(row_x, 32)], lambda by: res.at[rows(row_x, 32)])
+    last = [pair(1, res.at[rows(half, 128)], res.at[rows(half, 128)])]
+
+    def end_core():
+        arrive(first)
+        part[rows(half, 128)] += near[...]
+
+    def end_x():
+        arrive(over_x)
+        part[rows(row_x, 32)] += rx[0] + rx[1] + rx[2]
+
+    def end_y():
+        arrive(over_y)
+        part[rows(row_y, 8)] += ry[0] + ry[1] + ry[2]
+
+    def end_z():
+        arrive(over_z)
+        rz[me[2]] = part[rows(row_y, 8)]
+        res[rows(row_y, 8)] = (rz[0] + rz[1]) + (rz[2] + rz[3])
+
+    stages = [(first, end_core), (over_x, end_x), (over_y, end_y), (over_z, end_z),
+              (back_y, lambda: arrive(back_y)), (back_x, lambda: arrive(back_x)), (last, lambda: arrive(last))]
+
+    def drain():
+        for copies, _ in stages:
+            for copy in copies:
+                copy.wait_send()
+
+    return [(lambda c=copies: begin(c), end) for copies, end in stages], drain
+
+
+def all_reduce_scratch():
+    dma = pltpu.SemaphoreType.DMA
+    return [pltpu.VMEM((256, 256), F32), pltpu.VMEM((128, 256), F32), pltpu.VMEM((3, 32, 256), F32),
+            pltpu.VMEM((3, 8, 256), F32), pltpu.VMEM((4, 8, 256), F32),
+            dma((2,)), dma((2,)), dma((5, 3)), dma((5, 3))]
+
+
+def greet(peers):
+    barrier = pltpu.get_barrier_semaphore()
+    for p in peers:
+        pl.semaphore_signal(barrier, inc=1, device_id=p, device_id_type=MESH)
+    pl.semaphore_wait(barrier, len(peers))
+
+
+def all_peers(me, core):
+    return [device(shifted(me, a, s), core) for a in range(3) for s in (1, 2, 3)] + [device(me, 1 - core)]
+
+
+def reduce_kernel(fib, wt_own, kr, out, gram, fo, fp, wt_far, part, r1, r2, r3, tot,
+                  fo_sem, fs_sem, fr_sem, w_sem, s1, v1, s2, v2, s3, v3, *gram_scratch):
     me, core = position()
-    peers = [device(shifted(me, a, s), core) for a in range(3) for s in (1, 3)]
     partner = device(me, 1 - core)
-    barrier = pltpu.get_barrier_semaphore()
-    for p in peers + [partner]:
-        pl.semaphore_signal(barrier, inc=1, device_id=p, device_id_type=MESH)
-    pl.semaphore_wait(barrier, 7)
+    greet(all_peers(me, core))
+    gram_phases, gram_drain = all_reduce_phases(gram_scratch[0], gram, *gram_scratch[1:], me, core)
+
+    def gram_step(p):
+        gram_phases[p][1]()
+        if p < 6:
+            gram_phases[p + 1][0]()
 
     def column(t, k):
         x, y, z = block_at(t, me)
@@ -208,6 +294,9 @@
         rows16(c, body)
         msg2(1, d, c).start()
 
+    gram_scratch[0][...] = jnp.dot(wt_own[...], kr[...], preferred_element_type=F32)
+    gram_phases[0][0]()
+
     compute(0, MARKS[0])
     for c in range(3):
         for d in range(2):
@@ -216,6 +305,7 @@
     for c in range(3):
         for d in range(2):
             msg1(2, d, 0, c).start()
+    gram_step(0)
     compute(MARKS[1], 64)
 
     for i in range(4):
@@ -227,6 +317,7 @@
                 for c in range(3):
                     for d in range(2):
                         msg1(kind, d, i + 1, c).start()
+            gram_step(2 * i + 1)
         for c in range(3):
             finish1(i, c)
             if i == 0:
@@ -236,6 +327,8 @@
                 d = i - 1
                 msg2(2, d, c).start()
                 forward2(d, c)
+        if i < 3:
+            gram_step(2 * i + 2)
 
     for c in range(3):
         for d in range(2):
@@ -282,17 +375,19 @@
     def _(t):
         far_copy(t).wait_send()
 
-
-def reduce_rhs(fibers, weighted_t):
+    gram_drain()
+
+
+def reduce_rhs(fibers, weighted_t, kr_rows):
     cap = fibers.shape[0]
     dma = pltpu.SemaphoreType.DMA
     vmem = pltpu.VMEM
     return pl.pallas_call(
         reduce_kernel,
         name="reduce_rhs",
-        out_shape=jax.ShapeDtypeStruct((256, SUB), F32),
-        in_specs=[pl.BlockSpec(memory_space=pl.ANY), pl.BlockSpec(memory_space=pltpu.VMEM)],
-        out_specs=pl.BlockSpec(memory_space=pltpu.VMEM),
+        out_shape=(jax.ShapeDtypeStruct((256, SUB), F32), jax.ShapeDtypeStruct((256, 256), F32)),
+        in_specs=[pl.BlockSpec(memory_space=pl.ANY)] + [pl.BlockSpec(memory_space=pltpu.VMEM)] * 2,
+        out_specs=[pl.BlockSpec(memory_space=pltpu.VMEM)] * 2,
         scratch_shapes=[
             vmem((64, cap, SUB), BF16), vmem((64, cap, SUB), BF16), vmem((256, cap), BF16),
             vmem((4, 4, 4, 256, SUB), BF16),
@@ -300,10 +395,10 @@
             vmem((3, 2, 256, SUB // 2), F32), vmem((4, 256, SUB), F32),
             dma((64,)), dma((64,)), dma((64,)), dma((2,)),
             dma((3, 2, 4, 3)), dma((3, 2, 4, 3)), dma((3, 2, 3)), dma((3, 2, 3)), dma((3, 2, 3)), dma((3, 2, 3)),
-        ],
+        ] + all_reduce_scratch(),
         compiler_params=pltpu.CompilerParams(
             collective_id=0, has_side_effects=True, vmem_limit_bytes=60 * 1024 * 1024),
-    )(fibers, weighted_t)
+    )(fibers, weighted_t, kr_rows)
 
 
 def build_rows(factor_b, factor_c, row_b, mode3_idx, sample_wt, live):
@@ -314,16 +409,177 @@
     return (kr_rows, weighted)
 
 
-def contract_rows(left, right):
-    return lax.dot_general(left, right, (((0,), (0,)), ((), ())), preferred_element_type=F32)
-
-
-def inverse_of(matrix, ridge):
-    width = matrix.shape[0]
-    identity = jnp.eye(width, dtype=F32)
-    shifted_m = matrix + ridge * (jnp.trace(matrix) / width) * identity
-    lower = jnp.linalg.cholesky(shifted_m)
-    return jax.scipy.linalg.cho_solve((lower, True), identity)
+def dot32(a, b):
+    return jnp.dot(a, b, precision=lax.Precision.HIGHEST, preferred_element_type=F32)
+
+
+def dot16(a, b):
+    return jnp.dot(a.astype(BF16), b.astype(BF16), preferred_element_type=F32)
+
+
+def invert(a_ref, x_ref, r_ref):
+    n = a_ref.shape[0]
+    row = lax.broadcasted_iota(jnp.int32, (n, n), 0)
+    col = lax.broadcasted_iota(jnp.int32, (n, n), 1)
+    eye = jnp.where(row == col, F32(1), F32(0))
+    a = a_ref[...]
+    diag = jnp.where(row == col, a, F32(0))
+    s_col = lax.rsqrt(jnp.sum(diag, axis=1, keepdims=True))
+    s_row = lax.rsqrt(jnp.sum(diag, axis=0, keepdims=True))
+    a_ref[...] = a * s_col * s_row
+    bound = jnp.max(jnp.sum(jnp.abs(a_ref[...]), axis=0, keepdims=True))
+    alpha = 1.9 / bound
+    x_ref[...] = alpha * eye
+    r_ref[...] = eye - alpha * a_ref[...]
+
+    def coarse(carry):
+        it, _ = carry
+        r = r_ref[...]
+        x = x_ref[...]
+        x_ref[...] = x + dot16(x, r)
+        r = dot16(r, r)
+        r_ref[...] = r
+        return it + 1, jnp.sum(r * r)
+
+    lax.while_loop(lambda c: (c[0] < 24) & (c[1] > 1e-3), coarse, (jnp.int32(0), F32(1e9)))
+
+    def fine(carry):
+        it, last, _ = carry
+        x = x_ref[...]
+        e = (row == col).astype(F32) - dot32(a_ref[...], x)
+        size = jnp.sum(e * e)
+        reset = (it == 0) & jnp.logical_not(size < 0.25)
+        stop = (size < 1e-8) | ((size < 1e-3) & (size > 0.25 * last))
+
+        @pl.when(reset)
+        def _():
+            x_ref[...] = alpha * (row == col).astype(F32)
+
+        @pl.when(jnp.logical_not(reset))
+        def _():
+            x_ref[...] = x + dot32(x, e)
+
+        return it + 1, jnp.where(reset, F32(1e30), size), stop.astype(jnp.int32)
+
+    lax.while_loop(lambda c: (c[0] < 80) & (c[2] == 0), fine, (jnp.int32(0), F32(1e30), jnp.int32(0)))
+    x_ref[...] = x_ref[...] * s_col * s_row
+
+
+def solve_kernel(gram, rhs_t, factor, smat, shifted_m, work, inv, res):
+    n = gram.shape[0]
+    row = lax.broadcasted_iota(jnp.int32, (n, n), 0)
+    col = lax.broadcasted_iota(jnp.int32, (n, n), 1)
+    g = gram[...]
+    mean = jnp.sum(jnp.where(row == col, g, F32(0))) / n
+    a = g + jnp.where(row == col, ridge_share * mean, F32(0))
+    shifted_m[...] = a
+    work[...] = a
+    invert(work, inv, res)
+    r = rhs_t[...]
+    factor[...] = lax.dot_general(
+        r, inv[...], (((0,), (0,)), ((), ())), precision=lax.Precision.HIGHEST,
+        preferred_element_type=F32).astype(BF16)
+    smat[...] = lax.dot_general(
+        r, r, (((1,), (1,)), ((), ())), precision=lax.Precision.HIGHEST, preferred_element_type=F32)
+
+
+def solve_factor(gram, rhs_t):
+    square = jax.ShapeDtypeStruct((256, 256), F32)
+    return pl.pallas_call(
+        solve_kernel, name="solve_factor",
+        out_shape=(jax.ShapeDtypeStruct((SUB, 256), BF16), square, square),
+        scratch_shapes=[pltpu.VMEM((256, 256), F32)] * 3,
+    )(gram, rhs_t)
+
+
+def gather_kernel(own, smat, factor, ssum, x_s, x_v, c_s, c_v, *scratch):
+    me, core = position()
+    partner = device(me, 1 - core)
+    greet(all_peers(me, core))
+    work = scratch[0]
+    work[...] = smat[...]
+    phases, drain = all_reduce_phases(work, ssum, *scratch[1:], me, core)
+    phases[0][0]()
+
+    def block(x, k):
+        return factor.at[pl.ds(pl.multiple_of((2 * x + k) * SUB, SUB), SUB)]
+
+    over_x = [pltpu.make_async_remote_copy(
+        own, block(me[0], core), x_s.at[by - 1], x_v.at[by - 1],
+        device_id=device(shifted(me, 0, by), core), device_id_type=MESH) for by in (1, 2, 3)]
+    over_core = [pltpu.make_async_remote_copy(
+        own if by == 0 else block((me[0] + 4 - by) % 4, core), block((me[0] + 4 - by) % 4, core),
+        c_s.at[by], c_v.at[by], device_id=partner, device_id_type=MESH) for by in range(4)]
+    over_core[0].start()
+    phases[0][1]()
+    phases[1][0]()
+    for copy in over_x:
+        copy.start()
+    factor[pl.ds(pl.multiple_of((2 * me[0] + core) * SUB, SUB), SUB)] = own[...]
+    phases[1][1]()
+    for p in range(2, 5):
+        phases[p][0]()
+        phases[p][1]()
+    phases[5][0]()
+    for by in (1, 3, 2):
+        over_x[by - 1].wait_recv()
+        over_core[by].start()
+    phases[5][1]()
+    phases[6][0]()
+    phases[6][1]()
+    for by in range(4):
+        over_core[by].wait_recv()
+    for copy in over_x + over_core:
+        copy.wait_send()
+    drain()
+
+
+def gather_factor(own, smat):
+    dma = pltpu.SemaphoreType.DMA
+    vm = pl.BlockSpec(memory_space=pltpu.VMEM)
+    return pl.pallas_call(
+        gather_kernel, name="gather_factor",
+        out_shape=(jax.ShapeDtypeStruct((8 * SUB, 256), BF16), jax.ShapeDtypeStruct((256, 256), F32)),
+        in_specs=[vm, vm], out_specs=[vm, vm],
+        scratch_shapes=[dma((3,)), dma((3,)), dma((4,)), dma((4,))] + all_reduce_scratch(),
+        compiler_params=pltpu.CompilerParams(collective_id=1, has_side_effects=True),
+    )(own, smat)
+
+
+def leverage_kernel(scale, factor, smat, shifted_m, out, lev, work, inv, res):
+    work[...] = smat[...]
+    invert(work, inv, res)
+    a = shifted_m[...]
+    hinv = dot32(a, dot32(inv[...], a))
+    high = hinv.astype(BF16)
+    low = (hinv - high.astype(F32)).astype(BF16)
+    ones = jnp.full((8, 256), 1.0, BF16)
+    over = (((1,), (1,)), ((), ()))
+
+    @pl.loop(0, 8)
+    def _(j):
+        at = pl.ds(pl.multiple_of(j * SUB, SUB), SUB)
+        f = factor[at]
+        out[at] = f
+        quad = (jnp.dot(f, high, preferred_element_type=F32) + jnp.dot(f, low, preferred_element_type=F32)) * f.astype(F32)
+        q_high = quad.astype(BF16)
+        rest = quad - q_high.astype(F32)
+        q_mid = rest.astype(BF16)
+        q_low = (rest - q_mid.astype(F32)).astype(BF16)
+        total = (lax.dot_general(ones, q_high, over, preferred_element_type=F32)
+                 + lax.dot_general(ones, q_mid, over, preferred_element_type=F32)
+                 + lax.dot_general(ones, q_low, over, preferred_element_type=F32))
+        lev[j] = scale * total
+
+
+def leverage_of(factor, smat, shifted_m, scale):
+    rows = factor.shape[0]
+    out, lev = pl.pallas_call(
+        lambda *refs: leverage_kernel(scale, *refs), name="leverage",
+        out_shape=(jax.ShapeDtypeStruct((rows, 256), BF16), jax.ShapeDtypeStruct((rows // SUB, 8, SUB), F32)),
+        scratch_shapes=[pltpu.VMEM((256, 256), F32)] * 3,
+    )(factor, smat, shifted_m)
+    return out, lev[:, 0].reshape(rows).astype(BF16)
 
 
 def local(fibers, factor_b, factor_c, mode2_idx, mode3_idx, sample_wt, counts):
@@ -331,18 +587,10 @@
     rank_width = factor_c.shape[1]
     own_live = jnp.arange(slot_cap, dtype=jnp.int32) < counts[0]
     kr_rows, weighted = build_rows(factor_b, factor_c, mode2_idx, mode3_idx, sample_wt, own_live)
-    gram = lax.psum(contract_rows(weighted, kr_rows), ("blk", "row"))
-    gram_inv = inverse_of(gram, ridge_share)
-    rhs_t = reduce_rhs(fibers, weighted.T)
-    factor_own = lax.dot_general(
-        rhs_t, gram_inv, (((0,), (0,)), ((), ())), precision=lax.Precision.HIGHEST).astype(BF16)
-    factor = lax.all_gather(factor_own, "blk", axis=0, tiled=True)
-    smat = lax.psum(jnp.dot(rhs_t, rhs_t.T, precision=lax.Precision.HIGHEST), ("blk", "row"))
-    sinv = inverse_of(smat, 0.0)
-    quad = jnp.sum(jnp.dot(sinv, rhs_t, precision=lax.Precision.HIGHEST) * rhs_t, axis=0)
-    lev_own = ((row_total / rank_width) * quad).astype(BF16)
-    leverage = lax.all_gather(lev_own, "blk", axis=0, tiled=True)
-    return (factor, leverage)
+    rhs_t, gram = reduce_rhs(fibers, weighted.T, kr_rows)
+    factor_own, smat, shifted_m = solve_factor(gram, rhs_t)
+    factor, ssum = gather_factor(factor_own, smat)
+    return leverage_of(factor, ssum, shifted_m, row_total / rank_width)
 
 
 def solution(mesh):

time: 433 us -> 169 us (0.39)
  waiting for transfers between devices: 147 us -> 0 us
  other arithmetic: 125 us -> 2.16 us
  Pallas kernels: 99.4 us -> 159 us
  between operations: 19.4 us -> 1.49 us
  matrix products: 12.1 us -> 0 us
  blocking collectives: 11.6 us -> 0 us
  local copies, waits for them, and re-layouts: 17.3 us -> 6.71 us
    psum x1 -> x0, waiting for transfers between devices: 147 us -> none  [local(): gram = lax.psum(contract_rows(weighted, kr_rows), ('blk', 'row'))]
    another operation x19 -> x0, other arithmetic: 118 us -> none  [the longest x14 78.8 us: inverse_of(): lower = jnp.linalg.cholesky(shifted_m)]
    pallas_call x1 -> x4, Pallas kernels: 99.4 us -> 159 us  [the longest x1 107 us: reduce_rhs(): pl.pallas_call(reduce_kernel, name='reduce_rhs', out_shape=(jax.ShapeDtyp...]
    all_gather x1 -> x0, blocking collectives: 11.6 us -> none  [local(): leverage = lax.all_gather(lev_own, 'blk', axis=0, tiled=True)]
    another operation x19 -> x0, local copies, waits for them, and re-layouts: 8.1 us -> none  [the longest x15 8.05 us: inverse_of(): return jax.scipy.linalg.cho_solve((lower, True), identity)]
    another operation x16 -> x0, matrix products: 6.29 us -> none  [the longest x12 3.67 us: inverse_of(): return jax.scipy.linalg.cho_solve((lower, True), identity)]
    dot_general x4 -> x0, matrix products: 5.81 us -> none  [the longest x1 2.54 us: local(): jnp.dot(rhs_t, rhs_t.T, precision=lax.Precision.HIGHEST)]
  transfers between devices with their start and end apart: 2 -> 0, of which waited for: 1 -> 0; matrix products, arithmetic and copies ran while one was open for 12% -> 0% of each run, Pallas kernels for 0% -> 0%
where the time goes in v2:
time: 169 us
  Pallas kernels  159 us (94%)
  local copies, waits for them, and re-layouts  6.71 us (4%)
  other arithmetic  2.16 us (1%)
    pallas_call x1, Pallas kernels, reduce_rhs(): pl.pallas_call(reduce_kernel, name='reduce_rhs', out_shape=(jax.ShapeDtyp...  107 us
    pallas_call x1, Pallas kernels, gather_factor(): pl.pallas_call(gather_kernel, name='gather_factor', out_shape=(jax.ShapeD...  28.2 us
    pallas_call x1, Pallas kernels, leverage_of(): pl.pallas_call(lambda *refs: leverage_kernel(scale, *refs), name='leverag...  16.1 us
    pallas_call x1, Pallas kernels, solve_factor(): pl.pallas_call(solve_kernel, name='solve_factor', out_shape=(jax.ShapeDty...  7.1 us
    gather x2, local copies, waits for them, and re-layouts, build_rows(): product = factor_b[row_b].astype(F32) * factor_c[mode3_idx].astype(F32)  4.38 us

profile of v2, /device:TPU:1, one launch (start us, length us, event | category | flops | bytes accessed | tf_op | source)
XLA Modules:
  0.0 169.1 jit_solution(3179638019792768339)
XLA Ops:
  0.6 0.0 copy-start
  1.4 0.7 compare_select_fusion.2
  2.1 0.7 compare_select_fusion.1
  2.8 0.7 compare_select_fusion
  3.5 3.5 %gather_fusion = bf16[136,256]{1,0:T(8,128)(2,1)S(1)} fusion(bf16[8192,256]{1,0:T(8,128)(2,1)} %param.8, s32[1024]{0:T(1024)S(1)} %pad_clamp_fusion.1), kind=kCustom, calls=%fused_computation | custom fusion | bytes 139808 | tf_op jit(solution)/shard_map/gather | solution.py:405
  7.0 0.0 copy-done
  7.0 0.9 gather_fusion.1
  7.9 0.0 copy-start.1
  7.9 0.1 fusion
  8.0 0.8 copy.10.wt_own
  8.8 0.0 copy-done.1
  8.8 107.3 %reduce_rhs.1 = (f32[256,512]{1,0:T(8,128)}, f32[256,256]{1,0:T(8,128)}) custom-call(bf16[136,65536]{1,0:T(8,128)(2,1)} %fib.1, bf16[256,136]{1,0:T(8,128)(2,1)} %copy.10.wt_own, bf16[136,256]{1,0:T(8,128)(2,1)} %copy-done.1), custom_call_target="tpu_custom_call" | custom-call | tf_op jit(solution)/shard_map/reduce_rhs/pallas_call | solution.py:385
  116.1 7.1 %solve_factor.1 = (bf16[512,256]{1,0:T(8,128)(2,1)}, f32[256,256]{1,0:T(8,128)}, f32[256,256]{1,0:T(8,128)}) custom-call(f32[256,256]{1,0:T(8,128)} %get-tuple-element.11.gram, f32[256,512]{1,0:T(8,128)} %get-tuple-element.12.rhs_t), custom_call_target="tpu_custom_call" | custom-call | tf_op jit(solution)/shard_map/solve_factor/pallas_call | solution.py:488
  123.2 28.2 %gather_factor.1 = (bf16[4096,256]{1,0:T(8,128)(2,1)}, f32[256,256]{1,0:T(8,128)}) custom-call(bf16[512,256]{1,0:T(8,128)(2,1)} %get-tuple-element.13.own, f32[256,256]{1,0:T(8,128)} %get-tuple-element.14.smat), custom_call_target="tpu_custom_call" | custom-call | tf_op jit(solution)/shard_map/gather_factor/pallas_call | solution.py:540
  151.4 16.1 %leverage.1 = (bf16[4096,256]{1,0:T(8,128)(2,1)}, f32[8,8,512]{2,1,0:T(8,128)}) custom-call(bf16[4096,256]{1,0:T(8,128)(2,1)} %get-tuple-element.15.refs_0_, f32[256,256]{1,0:T(8,128)} %get-tuple-element.16.refs_1_, f32[256,256]{1,0:T(8,128)} %get-tuple-element.17.refs_2_), custom_call_target="tpu_custom_call" | custom-call | tf_op jit(solution)/shard_map/leverage/pallas_call | solution.py:577
  167.6 0.9 fusion.1
  168.5 0.6 copy.11
  (3 shorter events, 0.0 us)
Async XLA Ops:
  0.6 6.4 %copy-start = (bf16[4096,256]{1,0:T(8,128)(2,1)S(1)}, bf16[4096,256]{1,0:T(8,128)(2,1)}, u32[]{:S(2)}) copy-start(bf16[4096,256]{1,0:T(8,128)(2,1)} %param.9) | copy-start | bytes 6291460
  7.9 0.9 copy-start.1
